TPU v7x, 256 devices: a whole 4x4x8 slice. The times are simulated.
256 devices in a mesh: grid: 64 (over y, z, core), rep: 4 (over x).
Axes of the slice: x: 4, y: 4, z: 8, core: 2. Of those that a mesh axis runs over, the one named last changes fastest.
Arguments:
- integrals: bfloat16 [131072, 512], P(('grid', 'rep')), may hold values from -6 to 6
- green_occ: bfloat16 [512, 16384], P(None, 'grid'), may hold values from -0.25 to 0.25
- tile_panels: int32 [1024, 16], P(('grid', 'rep')), may hold values from 0 to 63, all different within a row; in each aligned block of 4 rows (0 to 3, 4 to 7, ...) at most 2 rows name the same one
- virtual_blocks: bfloat16 [64, 16, 256, 256], P('grid', 'rep'), may hold values from -0.0234375 to 0.0234375
Outputs:
- response_blocks: float32 [64, 128, 256], P('grid', 'rep')
Inputs may be any that keep to these rules, and one draw needn't show every extreme that they name: `tile_panels`: each row lists 16 different panels. In each aligned block of 4 rows (the tiles of one device) no panel is listed by more than 2 rows, and some panel is listed by exactly 2 rows.
All inputs are finite; a program needn't handle non-finite values.
Results may differ from a plain program's by a relative error of at most 0.0029.
Values may be sent and summed in bfloat16 or wider, within the bound.
A program may use at most 128 MiB of HBM per device.

v0:
```python
import jax
import jax.numpy as jnp
from jax import lax
from jax.sharding import PartitionSpec as P

CAP = 2


def shards(integrals, green_occ, tile_panels, virtual_blocks):
    grid_count = lax.axis_size("grid")
    tile_count = tile_panels.shape[0]
    tile_rows = integrals.shape[0] // tile_count
    panel_width = green_occ.shape[1]
    owners = jnp.arange(grid_count, dtype=jnp.int32)
    hit_count = jnp.sum(
        (tile_panels[:, :, None] == owners[None, None, :]).astype(jnp.int32), axis=1
    )
    before = jnp.cumsum(hit_count, axis=0) - hit_count
    slot_ids = jnp.arange(CAP, dtype=jnp.int32)
    placement = (hit_count[:, :, None] == 1) & (before[:, :, None] == slot_ids[None, None, :])
    place_weights = placement.astype(jnp.bfloat16)
    tile_ids = jnp.arange(tile_count, dtype=jnp.int32)
    labels = jnp.sum(placement.astype(jnp.int32) * tile_ids[:, None, None], axis=0)
    contracted = jnp.dot(
        integrals,
        lax.all_gather(green_occ, "grid", axis=1, tiled=True),
        preferred_element_type=jnp.float32,
    ).astype(jnp.bfloat16)
    tile_blocks = contracted.reshape(tile_count, tile_rows, grid_count, panel_width)
    outgoing = jnp.einsum(
        "ldc,ltdw->dctw", place_weights, tile_blocks, preferred_element_type=jnp.float32
    ).astype(jnp.bfloat16)
    arrived, got_labels = (
        lax.all_to_all(outgoing, "grid", split_axis=0, concat_axis=0, tiled=True),
        lax.all_to_all(labels, "grid", split_axis=0, concat_axis=0, tiled=True),
    )
    slot_owner = (got_labels[:, :, None] == tile_ids[None, None, :]).astype(jnp.bfloat16)
    summed = jnp.einsum("gcl,gctw->ltw", slot_owner, arrived, preferred_element_type=jnp.float32)
    owner_part = jnp.einsum(
        "ltw,lwc->tc",
        summed,
        virtual_blocks[0].astype(jnp.float32),
        precision=lax.Precision.HIGHEST,
    )
    return lax.psum_scatter(owner_part[None], "rep", scatter_dimension=1, tiled=True)


def solution(mesh):
    in_specs = (
        P(("grid", "rep"), None),
        P(None, "grid"),
        P(("grid", "rep"), None),
        P("grid", "rep", None, None),
    )
    out_specs = P("grid", "rep", None)
    return jax.shard_map(shards, mesh=mesh, in_specs=in_specs, out_specs=out_specs, check_vma=False)
```

profile of v0, /device:TPU:8, one launch (start us, length us, event | category | flops | bytes accessed | tf_op | source)
XLA Modules:
  0.0 416.4 jit_solution(14238982077939714297)
XLA Ops:
  6.5 0.0 copy-start
  6.5 0.0 all-gather.2.cloned.1.call-start
  6.5 0.7 all-gather.2.cloned.1.call-update
  7.3 0.8 convert_reduce_fusion
  8.1 0.7 copy.9
  8.8 12.1 %all-to-all-start = ((s32[64,1,2]{2,1,0:T(1,128)}), s32[64,1,2]{2,1,0:T(1,128)S(1)}, u32[]{:S(2)}, u32[]{:S(2)}) async-start(s32[64,1,2]{2,1,0:T(1,128)} %copy.9), calls=%async_computation | async-start | bytes 65536 | tf_op jit(solution)/shard_map/all_to_all | solution.py:35
  21.0 0.1 copy.15
  21.1 96.2 %all-gather.2.cloned.1.call-done = bf16[512,16384]{1,0:T(8,128)(2,1)} async-done(((bf16[512,256]{1,0:T(8,128)(2,1)}), bf16[512,16384]{1,0:T(8,128)(2,1)}) %all-gather.2.cloned.1.call-update) | async-done | bytes 16777232 | tf_op jit(solution)/shard_map/all_gather | solution.py:26
  117.3 0.0 copy-done
  117.3 18.0 %convolution_convert_fusion = bf16[512,16384]{1,0:T(8,128)(2,1)} fusion(bf16[512,512]{1,0:T(8,128)(2,1)S(1)} %copy-done, bf16[512,16384]{1,0:T(8,128)(2,1)} %all-gather.2.cloned.1.call-done), kind=kOutput, calls=%fused_computation | convolution fusion | flops 8598323200 | bytes 34078720 | tf_op jit(solution)/shard_map/dot_general | solution.py:24
  135.4 10.3 %copy.19 = bf16[64,8,64,256]{3,2,1,0:T(8,128)(2,1)S(1)} copy(bf16[64,8,64,256]{3,1,2,0:T(8,128)(2,1)} %bitcast.23) | data formatting | bytes 33554432
  145.6 0.0 copy-start.1
  145.6 35.7 %fusion.2 = bf16[64,2,128,256]{3,1,2,0:T(2,128)(2,1)} fusion(pred[4,64,2,1]{0,2,3,1:T(4,128)(4,1)S(1)} %copy.15, bf16[4,128,64,256]{3,2,1,0:T(8,128)(2,1)S(1)} %bitcast.22), kind=kOutput, calls=%fused_computation.3 | convolution fusion | flops 37748736 | bytes 25166336 | tf_op jit(solution)/shard_map/ldc,ltdw->dctw/dot_general | solution.py:30
  181.4 0.0 copy-start.2
  181.4 0.0 all-to-all-done
  181.4 9.3 %all-to-all-start.1 = ((bf16[64,2,128,256]{3,1,2,0:T(2,128)(2,1)}), bf16[64,2,128,256]{3,1,2,0:T(2,128)(2,1)}, u32[]{:S(2)}, u32[]{:S(2)}) async-start(bf16[64,2,128,256]{3,1,2,0:T(2,128)(2,1)} %fusion.2), calls=%async_computation.1 | async-start | bytes 16777216 | tf_op jit(solution)/shard_map/all_to_all | solution.py:34
  190.6 0.0 reduce-scatter.2.cloned.1.call-start
  190.7 0.1 copy.10
  190.8 184.1 %all-to-all-done.1 = bf16[64,2,128,256]{3,1,2,0:T(2,128)(2,1)} async-done(((bf16[64,2,128,256]{3,1,2,0:T(2,128)(2,1)}), bf16[64,2,128,256]{3,1,2,0:T(2,128)(2,1)}, u32[]{:S(2)}, u32[]{:S(2)}) %all-to-all-start.1) | async-done | bytes 8388640 | tf_op jit(solution)/shard_map/all_to_all | solution.py:34
  374.9 12.2 %fusion.7 = f32[4,128,256]{2,0,1:T(4,128)S(1)} fusion(bf16[64,2,128,256]{3,1,2,0:T(2,128)(2,1)} %all-to-all-done.1, s32[64,2]{0,1:T(2,128)S(1)} %bitcast.24), kind=kOutput, calls=%fused_computation.6 | convolution fusion | flops 33554944 | bytes 8913408 | tf_op jit(solution)/shard_map/gcl,gctw->ltw/dot_general | solution.py:38
  387.1 0.0 copy-done.2
  387.1 1.1 convolution_bitcast_fusion
  388.2 0.0 reduce-scatter.2.cloned.1.call-update
  388.2 21.4 %reduce-scatter.2.cloned.1.call-done = f32[1,32,256]{2,1,0:T(8,128)} async-done(((f32[1,128,256]{2,1,0:T(8,128)}), f32[1,32,256]{2,1,0:T(8,128)}) %reduce-scatter.2.cloned.1.call-update) | async-done | bytes 32784 | tf_op jit(solution)/shard_map/reduce_scatter | solution.py:45
  409.6 0.0 copy-done.1
  (5 shorter events, 0.1 us)
Async XLA Ops:
  6.5 110.8 %copy-start = (bf16[512,512]{1,0:T(8,128)(2,1)S(1)}, bf16[512,512]{1,0:T(8,128)(2,1)}, u32[]{:S(2)}) copy-start(bf16[512,512]{1,0:T(8,128)(2,1)} %param.4) | copy-start | bytes 1572868
  6.5 110.8 %all-gather.2.cloned.1.call-start = ((), (), s32[]{:S(2)}) async-start(), calls=%async_computation.3 | async-start | bytes 17039360 | tf_op jit(solution)/shard_map/all_gather | solution.py:26
  8.8 172.6 %all-to-all-start = ((s32[64,1,2]{2,1,0:T(1,128)}), s32[64,1,2]{2,1,0:T(1,128)S(1)}, u32[]{:S(2)}, u32[]{:S(2)}) async-start(s32[64,1,2]{2,1,0:T(1,128)} %copy.9), calls=%async_computation | async-start | bytes 65536 | tf_op jit(solution)/shard_map/all_to_all | solution.py:35
  145.6 264.0 %copy-start.1 = (bf16[512,512]{1,0:T(8,128)(2,1)S(1)}, bf16[512,512]{1,0:T(8,128)(2,1)}, u32[]{:S(2)}) copy-start(bf16[512,512]{1,0:T(8,128)(2,1)} %param.4) | copy-start | bytes 1572868
  181.4 205.7 %copy-start.2 = (bf16[1,4,256,256]{3,2,1,0:T(8,128)(2,1)S(1)}, bf16[1,4,256,256]{3,2,1,0:T(8,128)(2,1)}, u32[]{:S(2)}) copy-start(bf16[1,4,256,256]{3,2,1,0:T(8,128)(2,1)} %param.7) | copy-start | bytes 1572868
  181.4 193.5 %all-to-all-start.1 = ((bf16[64,2,128,256]{3,1,2,0:T(2,128)(2,1)}), bf16[64,2,128,256]{3,1,2,0:T(2,128)(2,1)}, u32[]{:S(2)}, u32[]{:S(2)}) async-start(bf16[64,2,128,256]{3,1,2,0:T(2,128)(2,1)} %fusion.2), calls=%async_computation.1 | async-start | bytes 16777216 | tf_op jit(solution)/shard_map/all_to_all | solution.py:34
  190.6 218.9 %reduce-scatter.2.cloned.1.call-start = ((), (), s32[]{:S(2)}) async-start(), calls=%async_computation.4 | async-start | bytes 163840 | tf_op jit(solution)/shard_map/reduce_scatter | solution.py:45
Sparse Core Ops, SparseCore 0:
  9.9 107.3 all-gather.1
  388.3 21.1 reduce-scatter.1
where the time goes:
time: 417 us; the launch traced here: 416 us
  waiting for transfers between devices  302 us (72%)
  matrix products  67.1 us (16%)
  starting transfers between devices  21.4 us (5%)
  between operations  13.5 us (3%)
  local copies, waits for them, and re-layouts  11.2 us (3%)
    all_to_all x1, waiting for transfers between devices, shards(): lax.all_to_all(outgoing, 'grid', split_axis=0, concat_axis=0, tiled=True)  184 us
    all_gather x1, waiting for transfers between devices, shards(): lax.all_gather(green_occ, 'grid', axis=1, tiled=True)  96.2 us
    dot_general x1, matrix products, shards(): jnp.einsum('ldc,ltdw->dctw', place_weights, tile_blocks, preferred_elemen...  35.7 us
    reduce_scatter x1, waiting for transfers between devices, shards(): lax.psum_scatter(owner_part[None], 'rep', scatter_dimension=1, tiled=True)  21.4 us
    dot_general x1, matrix products, shards(): jnp.dot(integrals, lax.all_gather(green_occ, 'grid', axis=1, tiled=True),...  18 us
    dot_general x1, matrix products, shards(): jnp.einsum('gcl,gctw->ltw', slot_owner, arrived, preferred_element_type=j...  12.2 us
    all_to_all x1, starting transfers between devices, shards(): lax.all_to_all(labels, 'grid', split_axis=0, concat_axis=0, tiled=True)  12.1 us
    unnamed x7, local copies, waits for them, and re-layouts  10.3 us
  transfers between devices with their start and end apart: 4, of which 3 were waited for; matrix products, arithmetic and copies ran while one was open for 16% of the time, Pallas kernels for 0%

commit v1 on v0

v1 whole, which is shorter than its diff:
```python
import jax
import jax.numpy as jnp
from jax import lax
from jax.experimental import pallas as pl
from jax.experimental.pallas import tpu as pltpu
from jax.sharding import PartitionSpec as P

NY, NZ, NC, NX = 4, 8, 2, 4
NP = NY * NC
F32, BF16 = jnp.float32, jnp.bfloat16


def body(a_hbm, g_hbm, tp_ref, v_hbm, out_ref,
         abuf, gbuf, tpbuf, vbuf, mask, part, stage, got, resp, xbuf,
         loc_sem, tp_s, tp_r, a_s, a_r, gz_s, gz_r, gx_s, gx_r, rs_s, rs_r, x_s, x_r):
    tiles, _, tr, _ = abuf.shape
    depth = gbuf.shape[1]
    half = tr // 2
    gi, r = lax.axis_index("grid"), lax.axis_index("rep")
    c, z, y = gi % NC, (gi // NC) % NZ, gi // (NC * NZ)
    me = y * NC + c

    def gid(yy, zz, cc):
        return (yy * NZ + zz) * NC + cc

    yl, yr, yo = (y + NY - 1) % NY, (y + 1) % NY, (y + 2) % NY
    partner = (gid(y, z, 1 - c), r)
    yp, ym = (gid(yr, z, c), r), (gid(yl, z, c), r)
    zp, zm = (gid(y, (z + 1) % NZ, c), r), (gid(y, (z + NZ - 1) % NZ, c), r)
    xs = [(gi, (r + d) % NX) for d in range(1, NX)]
    xp, xm = xs[0], xs[2]
    group = []
    for o in range(1, NP):
        q = (me + o) % NP
        group.append((gid(q // NC, z, q % NC), r))
    sends = []

    def send(src, dst, ss, rs, dev):
        copy = pltpu.make_async_remote_copy(
            src_ref=src, dst_ref=dst, send_sem=ss, recv_sem=rs,
            device_id=dev, device_id_type=pl.DeviceIdType.MESH)
        copy.start()
        sends.append(copy)

    def arrive(dst, ss, rs, dev):
        pltpu.make_async_remote_copy(
            src_ref=dst, dst_ref=dst, send_sem=ss, recv_sem=rs,
            device_id=dev, device_id_type=pl.DeviceIdType.MESH).wait_recv()

    local = [pltpu.make_async_copy(g_hbm, gbuf.at[z], loc_sem.at[tiles])]
    for l in range(tiles):
        local.append(pltpu.make_async_copy(a_hbm.at[l], abuf.at[l, me], loc_sem.at[l]))
    local.append(pltpu.make_async_copy(tp_ref, tpbuf.at[me], loc_sem.at[tiles + 1]))
    local.append(pltpu.make_async_copy(v_hbm, vbuf, loc_sem.at[tiles + 2]))
    for copy in local:
        copy.start()
    barrier = pltpu.get_barrier_semaphore()
    peers = group + [zp, zm] + xs
    for dev in peers:
        pl.semaphore_signal(barrier, inc=1, device_id=dev, device_id_type=pl.DeviceIdType.MESH)
    pl.semaphore_wait(barrier, len(peers))
    for copy in local:
        copy.wait()

    quarter = depth // 4
    par = r % 2

    def rows(parity, h):
        return pl.ds(pl.multiple_of((parity + 2 * h) * quarter, quarter), quarter)

    def g_send(way, k):
        d = k // 2
        zz = (z + NZ - d) % NZ if way == 0 else (z + d) % NZ
        h = k % 2 if k < 6 else way
        ref = gbuf.at[zz, rows(par, h)]
        send(ref, ref, gz_s.at[way, k], gz_r.at[way, k], zp if way == 0 else zm)

    def g_event(k):
        for way in (0, 1):
            d = k // 2 + 1
            zz = (z + NZ - d) % NZ if way == 0 else (z + d) % NZ
            h = k % 2 if k < 6 else way
            ref = gbuf.at[zz, rows(par, h)]
            arrive(ref, gz_s.at[way, k], gz_r.at[way, k], zp if way == 0 else zm)
            nxt = k + 2
            if nxt < 6:
                g_send(way, nxt)
            elif nxt in (6, 7) and h == way:
                g_send(way, 6)
            pidx = 6 if d == 4 else 2 * (d - 1) + way
            send(ref, ref, gx_s.at[h, pidx], gx_r.at[h, pidx], xp if h == 0 else xm)

    def g_side(pidx):
        d = pidx // 2 + 1
        zz = (z + NZ - d) % NZ if pidx % 2 == 0 else (z + d) % NZ
        for h in (0, 1):
            arrive(gbuf.at[zz, rows(1 - par, h)], gx_s.at[h, pidx], gx_r.at[h, pidx],
                   xp if h == 0 else xm)

    sl, sr, so = yl * NC + c, yr * NC + c, yo * NC + c
    ol, orr, oo, om = yl * NC + 1 - c, yr * NC + 1 - c, yo * NC + 1 - c, y * NC + 1 - c
    top, low = pl.ds(0, half), pl.ds(half, half)

    def a_send(l, slot, i, dev, cut=None):
        ref = abuf.at[l, slot] if cut is None else abuf.at[l, slot, cut]
        send(ref, ref, a_s.at[l, i], a_r.at[l, i], dev)

    def a_arrive(l, slot, i, dev, cut=None):
        ref = abuf.at[l, slot] if cut is None else abuf.at[l, slot, cut]
        arrive(ref, a_s.at[l, i], a_r.at[l, i], dev)

    def a_own(l):
        a_send(l, me, 0, yp)
        a_send(l, me, 1, ym)
        a_send(l, me, 4, partner)

    def a_hop(l):
        a_arrive(l, sl, 0, yp)
        a_send(l, sl, 2, yp, top)
        a_send(l, sl, 5, partner)
        a_arrive(l, sr, 1, ym)
        a_send(l, sr, 3, ym, low)
        a_send(l, sr, 6, partner)

    def a_far(l):
        a_arrive(l, so, 2, yp, top)
        a_send(l, so, 7, partner, top)
        a_arrive(l, so, 3, ym, low)
        a_send(l, so, 8, partner, low)

    def a_done(l):
        a_arrive(l, om, 4, partner)
        a_arrive(l, ol, 5, partner)
        a_arrive(l, orr, 6, partner)
        a_arrive(l, oo, 7, partner, top)
        a_arrive(l, oo, 8, partner, low)

    def masks():
        for o in range(1, NP):
            arrive(tpbuf.at[(me + NP - o) % NP], tp_s.at[o - 1], tp_r.at[o - 1], group[o - 1])
        tp = tpbuf[...].reshape(NP * 8, 128)
        lane = lax.broadcasted_iota(jnp.int32, (NP * 8, 128), 1)
        hit = jnp.zeros((NP * 8, 128), F32)
        for k in range(16):
            hit = hit + (tp[:, k:k + 1] == lane).astype(F32)
        row = lax.broadcasted_iota(jnp.int32, (128, NZ * 128), 0)
        col = lax.broadcasted_iota(jnp.int32, (128, NZ * 128), 1) // 128
        pick = (row == (y * NZ + col) * NC + c).astype(F32).astype(BF16)
        mask[...] = jnp.dot(hit.astype(BF16), pick, preferred_element_type=F32)

    def compute(l, dz):
        zz = (z + dz) % NZ
        lanes = pl.ds(pl.multiple_of(zz * 128, 128), 128)
        prod = jnp.dot(abuf[l].reshape(NP * tr, abuf.shape[3]), gbuf[zz],
                       preferred_element_type=F32).astype(BF16).astype(F32)
        total = None
        for s in range(NP):
            m = mask[pl.ds(s * 8 + l, 1), lanes]
            term = prod[s * tr:(s + 1) * tr] * jnp.concatenate([m, m], axis=1)
            total = term if total is None else total + term
        part[l, zz] = total

    def rs_step(l, t):
        for way in (0, 1):
            d = 4 - t
            zz = (z + d) % NZ if way == 0 else (z + NZ - d) % NZ
            dev = zp if way == 0 else zm
            cut = top if way == 0 else low
            if t == 0:
                stage[way, l, 0, cut] = part[l, zz, cut].astype(BF16)
                src, dst = stage.at[way, l, 0, cut], got.at[way, l, 0, cut]
            else:
                rs_wait(l, t - 1, way)
                if t == 1:
                    other = low if way == 0 else top
                    stage[way, l, 1, cut] = (part[l, zz, cut] + got[way, l, 0, cut].astype(F32)).astype(BF16)
                    stage[way, l, 1, other] = part[l, zz, other].astype(BF16)
                else:
                    stage[way, l, t] = (part[l, zz] + got[way, l, t - 1].astype(F32)).astype(BF16)
                src, dst = stage.at[way, l, t], got.at[way, l, t]
            send(src, dst, rs_s.at[way, l, t], rs_r.at[way, l, t], dev)

    def rs_wait(l, t, way):
        cut = top if way == 0 else low
        ref = got.at[way, l, t, cut] if t == 0 else got.at[way, l, t]
        arrive(ref, rs_s.at[way, l, t], rs_r.at[way, l, t], zp if way == 0 else zm)

    def finish(l):
        rs_wait(l, 3, 0)
        rs_wait(l, 3, 1)
        total = part[l, z] + got[0, l, 3].astype(F32) + got[1, l, 3].astype(F32)
        high = total.astype(BF16)
        rest = (total - high.astype(F32)).astype(BF16)
        value = (jnp.dot(high, vbuf[l], preferred_element_type=F32)
                 + jnp.dot(rest, vbuf[l], preferred_element_type=F32))
        resp[...] = value if l == 0 else resp[...] + value

    for k in range(2):
        for way in (0, 1):
            g_send(way, k)
    for o in range(1, NP):
        send(tpbuf.at[me], tpbuf.at[me], tp_s.at[o - 1], tp_r.at[o - 1], group[o - 1])
    a_own(0)
    a_own(1)
    g_event(0)
    g_event(1)
    a_hop(0)
    a_own(2)
    g_event(2)
    g_event(3)
    a_far(0)
    masks()
    a_hop(1)
    a_own(3)
    g_event(4)
    a_done(0)
    compute(0, 0)
    g_event(5)
    g_side(0)
    compute(0, -1 % NZ)
    g_side(1)
    compute(0, 1)
    a_far(1)
    g_event(6)
    g_side(2)
    compute(0, -2 % NZ)
    g_side(3)
    compute(0, 2)
    a_hop(2)
    g_side(4)
    compute(0, -3 % NZ)
    g_side(5)
    compute(0, 3)
    g_side(6)
    compute(0, 4)
    rs_step(0, 0)
    for l in range(1, tiles):
        a_done(l)
        compute(l, 4)
        rs_step(l, 0)
        if l + 1 < tiles:
            a_far(l + 1)
        compute(l, 3)
        compute(l, -3 % NZ)
        if l >= 2:
            rs_step(l - 2, 3)
        rs_step(l - 1, 1)
        compute(l, 2)
        compute(l, -2 % NZ)
        if l + 2 < tiles:
            a_hop(l + 2)
        compute(l, 1)
        compute(l, -1 % NZ)
        rs_step(l - 1, 2)
        if l >= 2:
            finish(l - 2)
        compute(l, 0)
    last = tiles - 1
    rs_step(last, 1)
    rs_step(last - 1, 3)
    rs_step(last, 2)
    finish(last - 1)
    rs_step(last, 3)
    finish(last)

    count = out_ref.shape[1]
    for d in range(1, NX):
        dst_r = (r + d) % NX
        send(resp.at[pl.ds(pl.multiple_of(dst_r * count, count), count)], xbuf.at[d - 1],
             x_s.at[d - 1], x_r.at[d - 1], xs[d - 1])
    total = resp[pl.ds(pl.multiple_of(r * count, count), count)]
    for d in range(1, NX):
        arrive(xbuf.at[d - 1], x_s.at[d - 1], x_r.at[d - 1], xs[d - 1])
        total = total + xbuf[d - 1]
    out_ref[0] = total
    for copy in sends:
        copy.wait_send()


def shards(integrals, green_occ, tile_panels, virtual_blocks):
    tiles = tile_panels.shape[0]
    tr = integrals.shape[0] // tiles
    depth, width = green_occ.shape
    cols = virtual_blocks.shape[3]
    tp = jnp.pad(tile_panels, ((0, 8 - tiles), (0, 128 - tile_panels.shape[1])), constant_values=-1)
    dma = pltpu.SemaphoreType.DMA
    anywhere = pl.BlockSpec(memory_space=pl.ANY)
    vmem = pl.BlockSpec(memory_space=pltpu.VMEM)
    return pl.pallas_call(
        body,
        out_shape=jax.ShapeDtypeStruct((1, tr // NX, cols), F32),
        in_specs=[anywhere, anywhere, vmem, anywhere],
        out_specs=vmem,
        scratch_shapes=[
            pltpu.VMEM((tiles, NP, tr, depth), BF16),
            pltpu.VMEM((NZ, depth, width), BF16),
            pltpu.VMEM((NP, 8, 128), jnp.int32),
            pltpu.VMEM((tiles, width, cols), BF16),
            pltpu.VMEM((NP * 8, NZ * 128), F32),
            pltpu.VMEM((tiles, NZ, tr, width), F32),
            pltpu.VMEM((2, tiles, 4, tr, width), BF16),
            pltpu.VMEM((2, tiles, 4, tr, width), BF16),
            pltpu.VMEM((tr, cols), F32),
            pltpu.VMEM((NX - 1, tr // NX, cols), F32),
            dma((tiles + 3,)),
            dma((NP - 1,)), dma((NP - 1,)),
            dma((tiles, 9)), dma((tiles, 9)),
            dma((2, 7)), dma((2, 7)),
            dma((2, 7)), dma((2, 7)),
            dma((2, tiles, 4)), dma((2, tiles, 4)),
            dma((NX - 1,)), dma((NX - 1,)),
        ],
        compiler_params=pltpu.CompilerParams(collective_id=0, has_side_effects=True),
    )(integrals.reshape(tiles, tr, depth), green_occ, tp, virtual_blocks[0])


def solution(mesh):
    in_specs = (
        P(("grid", "rep"), None),
        P(None, "grid"),
        P(("grid", "rep"), None),
        P("grid", "rep", None, None),
    )
    out_specs = P("grid", "rep", None)
    return jax.shard_map(shards, mesh=mesh, in_specs=in_specs, out_specs=out_specs, check_vma=False)
```

time: 417 us -> 75.7 us (0.18)
  waiting for transfers between devices: 302 us -> 0 us
  Pallas kernels: 0 us -> 72.6 us
  matrix products: 67.1 us -> 0 us
  starting transfers between devices: 21.4 us -> 0 us
  between operations: 13.5 us -> 0.01 us
  local copies, waits for them, and re-layouts: 11.2 us -> 2.65 us
    all_to_all x2 -> x0, waiting for transfers between devices: 184 us -> none  [the longest x1 184 us: shards(): lax.all_to_all(outgoing, 'grid', split_axis=0, concat_axis=0, tiled=True)]
    all_gather x1 -> x0, waiting for transfers between devices: 96.2 us -> none  [shards(): lax.all_gather(green_occ, 'grid', axis=1, tiled=True)]
    pallas_call x0 -> x1, Pallas kernels: none -> 72.6 us  [shards(): pl.pallas_call(body, out_shape=jax.ShapeDtypeStruct((1, tr // NX, cols),...]
    dot_general x4 -> x0, matrix products: 67.1 us -> none  [the longest x1 35.7 us: shards(): jnp.einsum('ldc,ltdw->dctw', place_weights, tile_blocks, preferred_elemen...]
    reduce_scatter x1 -> x0, waiting for transfers between devices: 21.4 us -> none  [shards(): lax.psum_scatter(owner_part[None], 'rep', scatter_dimension=1, tiled=True)]
    all_to_all x2 -> x0, starting transfers between devices: 21.4 us -> none  [the longest x1 12.1 us: shards(): lax.all_to_all(labels, 'grid', split_axis=0, concat_axis=0, tiled=True)]
    unnamed x7 -> x3, local copies, waits for them, and re-layouts: 10.3 us -> 2.06 us
  transfers between devices with their start and end apart: 4 -> 0, of which waited for: 3 -> 0; matrix products, arithmetic and copies ran while one was open for 16% -> 0% of each run, Pallas kernels for 0% -> 0%
where the time goes in v1:
time: 75.7 us; the launch traced here: 75.3 us
  Pallas kernels  72.6 us (96%)
  local copies, waits for them, and re-layouts  2.65 us (4%)
    pallas_call x1, Pallas kernels, shards(): pl.pallas_call(body, out_shape=jax.ShapeDtypeStruct((1, tr // NX, cols),...  72.6 us
    unnamed x3, local copies, waits for them, and re-layouts  2.06 us

profile of v1, /device:TPU:8, one launch (start us, length us, event | category | flops | bytes accessed | tf_op | source)
XLA Modules:
  0.0 75.3 jit_solution(2123946039745074463)
XLA Ops:
  0.0 0.0 copy-start
  0.0 0.7 copy-done
  0.7 0.6 pad.4.tp_ref
  1.3 72.6 %shard_map.46 = f32[1,32,256]{2,1,0:T(8,128)} custom-call(bf16[4,128,512]{2,1,0:T(8,128)(2,1)} %bitcast.2, bf16[512,256]{1,0:T(8,128)(2,1)} %g_hbm.1, s32[8,128]{1,0:T(8,128)} %pad.4.tp_ref, bf16[4,256,256]{2,1,0:T(8,128)(2,1)} %bitcast.3), custom_call_target="tpu_custom_call" | custom-call | tf_op jit(solution)/shard_map/pallas_call | solution.py:289
  73.9 1.4 %copy.6 = f32[1,32,256]{2,1,0:T(8,128)} copy(f32[1,32,256]{2,1,0:T(8,128)} %shard_map.46) | data formatting | bytes 65536
Async XLA Ops:
  0.0 0.7 copy-start

commit v2 on v1

--- a/solution.py
+++ b/solution.py
@@ -10,8 +10,8 @@
 F32, BF16 = jnp.float32, jnp.bfloat16
 
 
-def body(a_hbm, g_hbm, tp_ref, v_hbm, out_ref,
-         abuf, gbuf, tpbuf, vbuf, mask, part, stage, got, resp, xbuf,
+def body(a_hbm, g_hbm, tp_hbm, v_hbm, out_ref,
+         abuf, gbuf, tpbuf, vbuf, hits, mask, part, stage, got, resp, xbuf,
          loc_sem, tp_s, tp_r, a_s, a_r, gz_s, gz_r, gx_s, gx_r, rs_s, rs_r, x_s, x_r):
     tiles, _, tr, _ = abuf.shape
     depth = gbuf.shape[1]
@@ -50,12 +50,12 @@
     local = [pltpu.make_async_copy(g_hbm, gbuf.at[z], loc_sem.at[tiles])]
     for l in range(tiles):
         local.append(pltpu.make_async_copy(a_hbm.at[l], abuf.at[l, me], loc_sem.at[l]))
-    local.append(pltpu.make_async_copy(tp_ref, tpbuf.at[me], loc_sem.at[tiles + 1]))
+    local.append(pltpu.make_async_copy(tp_hbm, tpbuf.at[me], loc_sem.at[tiles + 1]))
     local.append(pltpu.make_async_copy(v_hbm, vbuf, loc_sem.at[tiles + 2]))
     for copy in local:
         copy.start()
     barrier = pltpu.get_barrier_semaphore()
-    peers = group + [zp, zm] + xs
+    peers = group + [zp, zm] + [(gid(y, (z + d) % NZ, c), r) for d in (2, NZ - 2)] + xs
     for dev in peers:
         pl.semaphore_signal(barrier, inc=1, device_id=dev, device_id_type=pl.DeviceIdType.MESH)
     pl.semaphore_wait(barrier, len(peers))
@@ -68,34 +68,42 @@
     def rows(parity, h):
         return pl.ds(pl.multiple_of((parity + 2 * h) * quarter, quarter), quarter)
 
+    def toward(way, d):
+        return (z + d) % NZ if way == 0 else (z + NZ - d) % NZ
+
+    def z_dev(way, d):
+        return (gid(y, toward(way, d), c), r)
+
+    far = (2, 2, 1, 1, 4, 3, 3)
+    jump = (2, 2, 1, 1, 2, 1, 1)
+
+    def g_half(way, k):
+        return way if k == 4 else (k + k // 5) % 2
+
     def g_send(way, k):
-        d = k // 2
-        zz = (z + NZ - d) % NZ if way == 0 else (z + d) % NZ
-        h = k % 2 if k < 6 else way
-        ref = gbuf.at[zz, rows(par, h)]
-        send(ref, ref, gz_s.at[way, k], gz_r.at[way, k], zp if way == 0 else zm)
+        ref = gbuf.at[toward(1 - way, far[k] - jump[k]), rows(par, g_half(way, k))]
+        send(ref, ref, gz_s.at[way, k], gz_r.at[way, k], z_dev(way, jump[k]))
 
     def g_event(k):
         for way in (0, 1):
-            d = k // 2 + 1
-            zz = (z + NZ - d) % NZ if way == 0 else (z + d) % NZ
-            h = k % 2 if k < 6 else way
-            ref = gbuf.at[zz, rows(par, h)]
-            arrive(ref, gz_s.at[way, k], gz_r.at[way, k], zp if way == 0 else zm)
-            nxt = k + 2
-            if nxt < 6:
-                g_send(way, nxt)
-            elif nxt in (6, 7) and h == way:
-                g_send(way, 6)
-            pidx = 6 if d == 4 else 2 * (d - 1) + way
-            send(ref, ref, gx_s.at[h, pidx], gx_r.at[h, pidx], xp if h == 0 else xm)
-
-    def g_side(pidx):
-        d = pidx // 2 + 1
-        zz = (z + NZ - d) % NZ if pidx % 2 == 0 else (z + d) % NZ
-        for h in (0, 1):
-            arrive(gbuf.at[zz, rows(1 - par, h)], gx_s.at[h, pidx], gx_r.at[h, pidx],
-                   xp if h == 0 else xm)
+            h = g_half(way, k)
+            ref = gbuf.at[toward(1 - way, far[k]), rows(par, h)]
+            arrive(ref, gz_s.at[way, k], gz_r.at[way, k], z_dev(way, jump[k]))
+            if k < 2:
+                if h == way:
+                    g_send(way, 4)
+                g_send(way, 5 + h)
+            send(ref, ref, gx_s.at[h, g_place(far[k], way)], gx_r.at[h, g_place(far[k], way)],
+                 xp if h == 0 else xm)
+
+    def g_place(d, way):
+        return 6 if d == 4 else 2 * (d - 1) + way
+
+    def g_side(d):
+        for way in (0, 1) if d < 4 else (0,):
+            for h in (0, 1):
+                arrive(gbuf.at[toward(1 - way, d), rows(1 - par, h)], gx_s.at[h, g_place(d, way)],
+                       gx_r.at[h, g_place(d, way)], xp if h == 0 else xm)
 
     sl, sr, so = yl * NC + c, yr * NC + c, yo * NC + c
     ol, orr, oo, om = yl * NC + 1 - c, yr * NC + 1 - c, yo * NC + 1 - c, y * NC + 1 - c
@@ -138,18 +146,26 @@
     def masks():
         for o in range(1, NP):
             arrive(tpbuf.at[(me + NP - o) % NP], tp_s.at[o - 1], tp_r.at[o - 1], group[o - 1])
-        tp = tpbuf[...].reshape(NP * 8, 128)
-        lane = lax.broadcasted_iota(jnp.int32, (NP * 8, 128), 1)
-        hit = jnp.zeros((NP * 8, 128), F32)
-        for k in range(16):
-            hit = hit + (tp[:, k:k + 1] == lane).astype(F32)
+        lane = lax.broadcasted_iota(jnp.int32, (tiles, 128), 1)
+        hits[...] = jnp.zeros_like(hits)
+        for s in range(NP):
+            tp = tpbuf[s]
+            hit = jnp.zeros((tiles, 128), F32)
+            for k in range(tp.shape[1]):
+                hit = hit + (tp[:, k:k + 1] == lane).astype(F32)
+            hits[s, pl.ds(0, tiles)] = hit
+        hit = hits[...].reshape(NP * 8, 128)
         row = lax.broadcasted_iota(jnp.int32, (128, NZ * 128), 0)
         col = lax.broadcasted_iota(jnp.int32, (128, NZ * 128), 1) // 128
         pick = (row == (y * NZ + col) * NC + c).astype(F32).astype(BF16)
         mask[...] = jnp.dot(hit.astype(BF16), pick, preferred_element_type=F32)
 
-    def compute(l, dz):
-        zz = (z + dz) % NZ
+    def compute(l, *panels):
+        for dz in panels:
+            one_panel(l, dz)
+
+    def one_panel(l, dz):
+        zz = (z + dz % NZ) % NZ
         lanes = pl.ds(pl.multiple_of(zz * 128, 128), 128)
         prod = jnp.dot(abuf[l].reshape(NP * tr, abuf.shape[3]), gbuf[zz],
                        preferred_element_type=F32).astype(BF16).astype(F32)
@@ -195,76 +211,54 @@
                  + jnp.dot(rest, vbuf[l], preferred_element_type=F32))
         resp[...] = value if l == 0 else resp[...] + value
 
-    for k in range(2):
-        for way in (0, 1):
-            g_send(way, k)
+    for k in range(tiles):
+        g_send(0, k)
+        g_send(1, k)
+        a_own(k)
     for o in range(1, NP):
         send(tpbuf.at[me], tpbuf.at[me], tp_s.at[o - 1], tp_r.at[o - 1], group[o - 1])
-    a_own(0)
-    a_own(1)
+    a_hop(0)
     g_event(0)
+    a_hop(1)
     g_event(1)
-    a_hop(0)
-    a_own(2)
     g_event(2)
+    a_hop(2)
     g_event(3)
+    masks()
+    a_hop(3)
+    g_event(4)
+    g_event(5)
     a_far(0)
-    masks()
-    a_hop(1)
-    a_own(3)
-    g_event(4)
+    g_event(6)
+    a_far(1)
+    a_far(2)
+    g_side(4)
     a_done(0)
-    compute(0, 0)
-    g_event(5)
-    g_side(0)
-    compute(0, -1 % NZ)
-    g_side(1)
-    compute(0, 1)
-    a_far(1)
-    g_event(6)
-    g_side(2)
-    compute(0, -2 % NZ)
-    g_side(3)
-    compute(0, 2)
-    a_hop(2)
-    g_side(4)
-    compute(0, -3 % NZ)
-    g_side(5)
-    compute(0, 3)
-    g_side(6)
     compute(0, 4)
     rs_step(0, 0)
+    a_far(3)
     for l in range(1, tiles):
         a_done(l)
         compute(l, 4)
         rs_step(l, 0)
-        if l + 1 < tiles:
-            a_far(l + 1)
-        compute(l, 3)
-        compute(l, -3 % NZ)
-        if l >= 2:
-            rs_step(l - 2, 3)
-        rs_step(l - 1, 1)
-        compute(l, 2)
-        compute(l, -2 % NZ)
-        if l + 2 < tiles:
-            a_hop(l + 2)
-        compute(l, 1)
-        compute(l, -1 % NZ)
-        rs_step(l - 1, 2)
-        if l >= 2:
-            finish(l - 2)
+    g_side(3)
+    for l in range(tiles):
+        compute(l, 3, -3)
+        rs_step(l, 1)
+    g_side(2)
+    for l in range(tiles):
+        compute(l, 2, -2)
+        rs_step(l, 2)
+    g_side(1)
+    for l in range(tiles):
+        compute(l, 1, -1)
+        rs_step(l, 3)
+    for l in range(tiles):
         compute(l, 0)
-    last = tiles - 1
-    rs_step(last, 1)
-    rs_step(last - 1, 3)
-    rs_step(last, 2)
-    finish(last - 1)
-    rs_step(last, 3)
-    finish(last)
+        finish(l)
 
     count = out_ref.shape[1]
-    for d in range(1, NX):
+    for d in (2, 1, 3):
         dst_r = (r + d) % NX
         send(resp.at[pl.ds(pl.multiple_of(dst_r * count, count), count)], xbuf.at[d - 1],
              x_s.at[d - 1], x_r.at[d - 1], xs[d - 1])
@@ -282,20 +276,20 @@
     tr = integrals.shape[0] // tiles
     depth, width = green_occ.shape
     cols = virtual_blocks.shape[3]
-    tp = jnp.pad(tile_panels, ((0, 8 - tiles), (0, 128 - tile_panels.shape[1])), constant_values=-1)
     dma = pltpu.SemaphoreType.DMA
     anywhere = pl.BlockSpec(memory_space=pl.ANY)
     vmem = pl.BlockSpec(memory_space=pltpu.VMEM)
     return pl.pallas_call(
         body,
         out_shape=jax.ShapeDtypeStruct((1, tr // NX, cols), F32),
-        in_specs=[anywhere, anywhere, vmem, anywhere],
+        in_specs=[anywhere] * 4,
         out_specs=vmem,
         scratch_shapes=[
             pltpu.VMEM((tiles, NP, tr, depth), BF16),
             pltpu.VMEM((NZ, depth, width), BF16),
-            pltpu.VMEM((NP, 8, 128), jnp.int32),
+            pltpu.VMEM((NP,) + tile_panels.shape, jnp.int32),
             pltpu.VMEM((tiles, width, cols), BF16),
+            pltpu.VMEM((NP, 8, 128), F32),
             pltpu.VMEM((NP * 8, NZ * 128), F32),
             pltpu.VMEM((tiles, NZ, tr, width), F32),
             pltpu.VMEM((2, tiles, 4, tr, width), BF16),
@@ -311,7 +305,7 @@
             dma((NX - 1,)), dma((NX - 1,)),
         ],
         compiler_params=pltpu.CompilerParams(collective_id=0, has_side_effects=True),
-    )(integrals.reshape(tiles, tr, depth), green_occ, tp, virtual_blocks[0])
+    )(integrals.reshape(tiles, tr, depth), green_occ, tile_panels, virtual_blocks[0])
 
 
 def solution(mesh):

time: 75.7 us -> 59.3 us (0.78)
  Pallas kernels: 72.6 us -> 57.4 us
  local copies, waits for them, and re-layouts: 2.65 us -> 1.38 us
    pallas_call x1, Pallas kernels: 72.6 us -> 57.4 us  [shards(): pl.pallas_call(body, out_shape=jax.ShapeDtypeStruct((1, tr // NX, cols),...]
    unnamed x3 -> x1, local copies, waits for them, and re-layouts: 2.06 us -> 1.38 us
where the time goes in v2:
time: 59.3 us; the launch traced here: 58.7 us
  Pallas kernels  57.4 us (97%)
  local copies, waits for them, and re-layouts  1.38 us (2%)
    pallas_call x1, Pallas kernels, shards(): pl.pallas_call(body, out_shape=jax.ShapeDtypeStruct((1, tr // NX, cols),...  57.4 us
    unnamed x1, local copies, waits for them, and re-layouts  1.38 us

profile of v2, /device:TPU:8, one launch (start us, length us, event | category | flops | bytes accessed | tf_op | source)
XLA Modules:
  0.0 58.7 jit_solution(1140873502993131390)
XLA Ops:
  0.0 57.4 %shard_map.46 = f32[1,32,256]{2,1,0:T(8,128)} custom-call(bf16[4,128,512]{2,1,0:T(8,128)(2,1)} %bitcast.2, bf16[512,256]{1,0:T(8,128)(2,1)} %g_hbm.1, s32[4,16]{1,0:T(4,128)} %tp_hbm.1, bf16[4,256,256]{2,1,0:T(8,128)(2,1)} %bitcast.3), custom_call_target="tpu_custom_call" | custom-call | tf_op jit(solution)/shard_map/pallas_call | solution.py:282
  57.4 1.4 %copy.6 = f32[1,32,256]{2,1,0:T(8,128)} copy(f32[1,32,256]{2,1,0:T(8,128)} %shard_map.46) | data formatting | bytes 65536
